TPU v7x, 512 devices: a whole 4x8x8 slice. The times are simulated.
512 devices in a mesh: row: 32 (over y, x_hi, core), col: 16 (over x_lo, z).
Axes of the slice: x: 4 (x_hi: 2, x_lo: 2; x = x_hi * 2 + x_lo), y: 8, z: 8, core: 2. Of those that a mesh axis runs over, the one named last changes fastest.
Arguments:
- tile_blocks: bfloat16 [12288, 128, 128], P(('row', 'col')), may hold values from -0.21875 to 0.21875
- tile_rows: int32 [12288], P(('row', 'col')), may hold values from 0 to 4095, as said below
- tile_cols: int32 [12288], P(('row', 'col')), may hold values from 0 to 4095, as said below
- trial_vectors: bfloat16 [4, 524288], P(None, ('col', 'row')), may hold values from -6 to 6
- basis_old: float32 [44, 524288], P(None, ('col', 'row'))
- image_old: float32 [44, 524288], P(None, ('col', 'row'))
Outputs:
- projected: float32 [48, 48], replicated
- basis_new: float32 [48, 524288], P(None, ('col', 'row'))
- image_new: float32 [48, 524288], P(None, ('col', 'row'))
Inputs may be any that keep to these rules, and one draw needn't show every extreme that they name: `tile_rows`: the 24 tiles of each device with index r on row have block rows b for which (b // 8) % 32 equals r. `tile_cols`: the 24 tiles of each device with index c on col have block columns from c * 256 to (c + 1) * 256 - 1.
All inputs are finite; a program needn't handle non-finite values.
Results may differ from a plain program's by a relative error of at most 0.0003.
Values may be sent and summed in bfloat16 or wider, within the bound.
A program may use at most 64 MiB of HBM per device.

v0:
```python
import jax
import jax.numpy as jnp
from jax import lax
from jax.sharding import PartitionSpec as P


def rows_product(left, right):
    return lax.dot_general(left, right, (((1,), (1,)), ((), ())), precision=lax.Precision.HIGHEST)


def place_blocks(local_index, block_count, products):
    onehot = (local_index[None, :] == jnp.arange(block_count, dtype=jnp.int32)[:, None]).astype(
        jnp.float32
    )
    flat = products.reshape(products.shape[0], -1)
    placed = jnp.dot(onehot, flat, precision=lax.Precision.HIGHEST)
    return placed.reshape(block_count, products.shape[1], products.shape[2])


def local(tile_blocks, tile_rows, tile_cols, trial_vectors, basis_old, image_old):
    tile_size = tile_blocks.shape[1]
    piece_width = trial_vectors.shape[1]
    vec_count = trial_vectors.shape[0]
    blocks_dev = piece_width // tile_size
    n_row = lax.axis_size("row")
    n_col = lax.axis_size("col")
    row_blocks = blocks_dev * n_col
    col_blocks = blocks_dev * n_row
    row_index = lax.axis_index("row")
    col_index = lax.axis_index("col")
    all_rows = float(piece_width * n_row * n_col)
    gathered = lax.all_gather(trial_vectors, ("row", "col"), axis=1, tiled=True)
    grid = gathered.reshape(vec_count, n_row, n_col, piece_width)
    col_vectors = lax.dynamic_index_in_dim(grid, col_index, 2, keepdims=False).reshape(
        vec_count, -1
    )
    row_vectors = lax.dynamic_index_in_dim(grid, row_index, 1, keepdims=False).reshape(
        vec_count, -1
    )
    local_rows = tile_rows // blocks_dev // n_row * blocks_dev + tile_rows % blocks_dev
    local_cols = tile_cols - col_index * col_blocks
    picked_cols = jnp.take(
        col_vectors.reshape(vec_count, col_blocks, tile_size), local_cols, axis=1
    )
    forward = jnp.einsum(
        "ktb,tab->tka", picked_cols, tile_blocks, preferred_element_type=jnp.float32
    )
    picked_rows = jnp.take(
        row_vectors.reshape(vec_count, row_blocks, tile_size), local_rows, axis=1
    )
    backward = jnp.einsum(
        "kta,tab->tkb", picked_rows, tile_blocks, preferred_element_type=jnp.float32
    )
    row_partial = place_blocks(local_rows, row_blocks, forward)
    col_partial = place_blocks(local_cols, col_blocks, backward)
    col_share = lax.psum_scatter(col_partial, "row", scatter_dimension=0, tiled=True)
    row_total = lax.psum(row_partial, "col")
    own_rows = lax.dynamic_slice_in_dim(row_total, col_index * blocks_dev, blocks_dev, 0)
    new_image = (own_rows + col_share).transpose(1, 0, 2).reshape(vec_count, piece_width)
    trial_wide = trial_vectors.astype(jnp.float32)
    basis_all = jnp.concatenate([basis_old, trial_wide], axis=0)
    images_all = jnp.concatenate([image_old, new_image], axis=0)
    correlation, coupling = lax.psum(
        (rows_product(basis_all, basis_all), rows_product(basis_all, images_all)), ("row", "col")
    )
    correlation = correlation / all_rows
    coupling = coupling / all_rows
    factor = jnp.linalg.cholesky(correlation)

    def solve_lower(matrix):
        return lax.linalg.triangular_solve(factor, matrix, left_side=True, lower=True)

    half_done = solve_lower(coupling)
    projected = solve_lower(half_done.T).T
    return (projected, solve_lower(basis_all), solve_lower(images_all))


def solution(mesh):
    in_specs = (
        P(("row", "col"), None, None),
        P(("row", "col")),
        P(("row", "col")),
        P(None, ("col", "row")),
        P(None, ("col", "row")),
        P(None, ("col", "row")),
    )
    out_specs = (P(), P(None, ("col", "row")), P(None, ("col", "row")))
    return jax.shard_map(local, mesh=mesh, in_specs=in_specs, out_specs=out_specs, check_vma=False)
```

profile of v0, /device:TPU:1, one launch (start us, length us, event | category | flops | bytes accessed | tf_op | source)
XLA Modules:
  0.0 1796.1 jit_solution(15084369518175985899)
XLA Ops:
  7.2 0.0 copy-start
  7.2 0.0 all-gather.2.cloned.1.call-start
  7.2 0.7 all-gather.2.cloned.1.call-update
  7.9 0.0 all-reduce.3.cloned.1.call-start
  8.0 0.7 compare_and_fusion
  8.7 1393.4 %all-gather.2.cloned.1.call-done = bf16[4,524288]{1,0:T(4,128)(2,1)} async-done(((bf16[4,1024]{1,0:T(4,128)(2,1)}), bf16[4,524288]{1,0:T(4,128)(2,1)}) %all-gather.2.cloned.1.call-update) | async-done | bytes 4194320 | tf_op jit(solution)/shard_map/all_gather | solution.py:32
  1402.1 3.6 copy.35
  1405.7 0.0 copy-start.1
  1405.7 0.0 copy-start.4
  1405.7 0.0 copy-start.2
  1405.7 0.0 copy-start.3
  1405.7 1.9 copy-done.1
  1407.6 1.5 dynamic-slice_reduce_fusion
  1409.2 0.1 reshape_reshape.6
  1409.3 0.2 copy.22
  1409.5 0.6 gather_fusion
  1410.1 0.0 copy-done
  1410.1 0.5 fusion.13
  1410.6 1.1 fusion.7
  1411.7 0.0 all-reduce.3.cloned.1.call-update
  1411.8 0.0 reduce-scatter.2.cloned.1.call-start
  1411.8 0.9 dynamic-slice_bitcast_fusion
  1412.7 0.1 reshape_reshape.7
  1412.8 0.1 copy.25
  1412.9 0.6 gather_fusion.1
  1413.5 0.4 fusion.11
  1413.9 1.3 fusion.4
  1415.2 0.0 reduce-scatter.2.cloned.1.call-update
  1415.2 0.0 copy-done.4
  1415.2 0.0 copy-done.2
  1415.2 0.3 fusion.3
  1415.5 128.8 %all-reduce.3.cloned.1.call-done = f32[128,4,128]{2,0,1:T(8,128)} async-done(((f32[128,4,128]{2,0,1:T(8,128)}), f32[128,4,128]{2,0,1:T(8,128)}) %all-reduce.3.cloned.1.call-update) | async-done | bytes 262160 | tf_op jit(solution)/shard_map/psum | solution.py:57
  1544.3 129.5 %reduce-scatter.2.cloned.1.call-done = f32[8,4,128]{2,0,1:T(8,128)} async-done(((f32[256,4,128]{2,0,1:T(8,128)}), f32[8,4,128]{2,0,1:T(8,128)}) %reduce-scatter.2.cloned.1.call-update) | async-done | bytes 16400 | tf_op jit(solution)/shard_map/reduce_scatter | solution.py:56
  1673.8 0.7 add_bitcast_fusion
  1674.5 0.0 copy-done.3
  1674.6 0.3 fusion.1
  1674.9 102.0 %all-reduce = (f32[48,48]{0,1:T(8,128)S(1)}, f32[48,48]{0,1:T(8,128)S(1)}) all-reduce(f32[48,48]{0,1:T(8,128)S(1)} %fusion.3, f32[48,48]{0,1:T(8,128)S(1)} %fusion.1), channel_id=1, replica_groups=mesh['row'=32,'col'=16] {'row','col'}, use_global_device_ids=true, to_apply=%region_0.1 | all-reduce | flops 4608 | bytes 36864 | tf_op jit(solution)/shard_map/psum | solution.py:63
  1776.9 0.1 copy.20
  1777.0 4.4 cholesky.18
  1781.4 0.6 compare_reduce_fusion
  1782.0 0.7 fusion.10
  1782.7 3.7 custom-call.12
  1786.4 1.1 fusion
  1787.4 1.0 fusion.2
  1788.5 0.2 convolution_bitcast_fusion.1
  1788.7 0.2 convolution_bitcast_fusion
  1788.9 0.7 copy.28
  (9 shorter events, 0.1 us)
Async XLA Ops:
  7.2 1402.9 %copy-start = (bf16[24,128,128]{2,1,0:T(8,128)(2,1)S(1)}, bf16[24,128,128]{2,1,0:T(8,128)(2,1)}, u32[]{:S(2)}) copy-start(bf16[24,128,128]{2,1,0:T(8,128)(2,1)} %param.10) | copy-start | bytes 2359300
  7.2 1394.9 %all-gather.2.cloned.1.call-start = ((), (), s32[]{:S(2)}) async-start(), calls=%async_computation.1 | async-start | bytes 4202496 | tf_op jit(solution)/shard_map/all_gather | solution.py:32
  7.9 1536.4 %all-reduce.3.cloned.1.call-start = ((), (), s32[]{:S(2)}) async-start(), calls=%async_computation.2 | async-start | bytes 524288 | tf_op jit(solution)/shard_map/psum | solution.py:57
  1405.7 1.9 copy-start.1
  1405.7 9.5 copy-start.4
  1405.7 9.5 copy-start.2
  1405.7 268.8 %copy-start.3 = (f32[44,1024]{1,0:T(8,128)S(1)}, f32[44,1024]{1,0:T(8,128)}, u32[]{:S(2)}) copy-start(f32[44,1024]{1,0:T(8,128)} %param.15) | copy-start | bytes 540676
  1411.8 262.0 %reduce-scatter.2.cloned.1.call-start = ((), (), s32[]{:S(2)}) async-start(), calls=%async_computation.3 | async-start | bytes 540672 | tf_op jit(solution)/shard_map/reduce_scatter | solution.py:56
Sparse Core Ops, SparseCore 0:
  10.2 1391.8 all-gather.1
  1411.9 132.4 all-reduce.2
  1549.6 124.1 reduce-scatter.1
where the time goes:
time: 1800 us
  waiting for transfers between devices  1650 us (92%)
  blocking collectives  102 us (6%)
    all_gather x1, waiting for transfers between devices, local(): gathered = lax.all_gather(trial_vectors, ('row', 'col'), axis=1, tiled=True)  1390 us
    reduce_scatter x1, waiting for transfers between devices, local(): lax.psum_scatter(col_partial, 'row', scatter_dimension=0, tiled=True)  129 us
    psum x1, waiting for transfers between devices, local(): row_total = lax.psum(row_partial, 'col')  129 us
    psum x1, blocking collectives, local(): lax.psum((rows_product(basis_all, basis_all), rows_product(basis_all, ima...  102 us
  transfers between devices with their start and end apart: 3, of which 3 were waited for; matrix products, arithmetic and copies ran while one was open for 0% of the time, Pallas kernels for 0%

commit v1 on v0

v1 whole, which is shorter than its diff:
```python
import functools

import jax
import jax.numpy as jnp
from jax import lax
from jax.experimental import pallas as pl
from jax.experimental.pallas import tpu as pltpu
from jax.sharding import PartitionSpec as P

MESH = pl.DeviceIdType.MESH
F32 = jnp.float32
BF16 = jnp.bfloat16
HIGHEST = lax.Precision.HIGHEST


def dot_nt(a, b):
    return lax.dot_general(a, b, (((1,), (1,)), ((), ())), precision=HIGHEST, preferred_element_type=F32)


def dot_nn(a, b):
    return lax.dot_general(a, b, (((1,), (0,)), ((), ())), precision=HIGHEST, preferred_element_type=F32)


def lower_inverse(a):
    n = a.shape[0]
    tiles = n // 8
    sub = lax.broadcasted_iota(jnp.int32, (8, n), 0)
    lane = lax.broadcasted_iota(jnp.int32, (8, n), 1)
    left = [a[8 * i : 8 * i + 8, :] for i in range(tiles)]
    right = [jnp.where(sub + 8 * i == lane, 1.0, 0.0).astype(F32) for i in range(tiles)]
    for j in range(n):
        at, row = j // 8, j % 8
        pivot_left = left[at][row : row + 1, :]
        pivot_right = right[at][row : row + 1, :]
        inv = 1.0 / pivot_left[:, j : j + 1]
        pivot_left = pivot_left * inv
        pivot_right = pivot_right * inv
        for i in range(at, tiles):
            ratio = left[i][:, j : j + 1]
            if i == at:
                ratio = jnp.where(sub[:, :1] > row, ratio, 0.0)
            left[i] = left[i] - ratio * pivot_left
            right[i] = right[i] - ratio * pivot_right
    out = []
    for i in range(tiles):
        diag = jnp.sum(jnp.where(sub + 8 * i == lane, left[i], 0.0), axis=1, keepdims=True)
        out.append(right[i] / jnp.sqrt(diag))
    return jnp.concatenate(out, axis=0)


def kernel(
    n_row, n_col, total_cols,
    rows_s, cols_s, tiles_h, trial_h, basis_h, image_h,
    proj_o, basis_o, image_o,
    tiles, trial, old_basis, old_image, basis, image, mix,
    x_row, x_col, prod, row_send, col_send, row_recv, col_recv,
    gram, e1, e2, e3, late, a1, a2, new_basis, new_image, proj,
    loc, sem,
):
    r = lax.axis_index("row")
    c = lax.axis_index("col")
    n_old = basis_h.shape[0]
    n_vec = trial_h.shape[0]
    n_all = n_old + n_vec
    kt = tiles.shape[0]
    n_y = n_row // 4
    y, q = r // 4, r % 4

    local = [
        pltpu.make_async_copy(trial_h, trial, loc.at[0]),
        pltpu.make_async_copy(basis_h, old_basis, loc.at[1]),
        pltpu.make_async_copy(image_h, old_image, loc.at[2]),
        pltpu.make_async_copy(tiles_h, tiles, loc.at[3]),
    ]
    for copy in local:
        copy.start()

    bar = pltpu.get_barrier_semaphore()

    @pl.loop(1, n_row)
    def _(d):
        pl.semaphore_signal(bar, 1, device_id=(lax.rem(r + d, n_row), c), device_id_type=MESH)

    @pl.loop(1, n_col)
    def _(d):
        pl.semaphore_signal(bar, 1, device_id=(r, lax.rem(c + d, n_col)), device_id_type=MESH)

    local[0].wait()
    for j in range(8):
        block = trial[:, 128 * j : 128 * (j + 1)]
        x_row[r * 8 + j] = block
        x_col[c * 8 + j] = block
    pl.semaphore_wait(bar, n_row + n_col - 2)

    def rcopy(src, dst, k, dev):
        return pltpu.make_async_remote_copy(
            src, dst, sem.at[k, 0], sem.at[k, 1], device_id=dev, device_id_type=MESH
        )

    def drain(view, k):
        w = rcopy(view, view, k, (r, c))
        w.wait_send()
        w.wait_recv()

    @pl.loop(1, n_row)
    def _(d):
        own = pl.ds(r * 8, 8)
        rcopy(x_row.at[own], x_row.at[own], 0, (lax.rem(r + d, n_row), c)).start()

    @pl.loop(1, n_col)
    def _(d):
        own = pl.ds(c * 8, 8)
        rcopy(x_col.at[own], x_col.at[own], 1, (r, lax.rem(c + d, n_col))).start()

    local[1].wait()
    local[2].wait()
    basis[0:n_old, :] = old_basis[...]
    image[0:n_old, :] = old_image[...]
    basis[n_old:n_all, :] = trial[...].astype(F32)
    image[n_old:n_all, :] = jnp.zeros((n_vec, image.shape[1]), F32)
    mix[0:n_all, :] = basis[...]
    mix[n_all : 2 * n_all, :] = image[...]
    g = dot_nt(basis[...], mix[...])
    gram[...] = jnp.zeros(gram.shape, F32)
    for i in range(n_all // 8):
        gram[i, :, 0 : 2 * n_all] = g[8 * i : 8 * i + 8, :]

    e1[y] = gram[y]

    @pl.loop(1, n_y)
    def _(d):
        to = lax.rem(y + d, n_y)
        rcopy(gram.at[to], e1.at[y], 2, (to * 4 + q, c)).start()

    local[3].wait()
    drain(x_row.at[pl.ds(0, (n_row - 1) * 8)], 0)
    drain(x_col.at[pl.ds(0, (n_col - 1) * 8)], 1)

    def row_of(t):
        b = rows_s[t]
        return b // (8 * n_row) * 8 + b % 8

    def col_of(t):
        return cols_s[t] % (8 * n_row)

    prod[...] = jnp.zeros(prod.shape, F32)

    @pl.loop(0, kt // 4)
    def _(s):
        fwd, bwd = [], []
        for u in range(4):
            t = s * 4 + u
            tile = tiles[t]
            fwd.append(
                lax.dot_general(x_row[col_of(t)], tile, (((1,), (1,)), ((), ())), preferred_element_type=F32)
            )
            bwd.append(
                lax.dot_general(x_col[row_of(t)], tile, (((1,), (0,)), ((), ())), preferred_element_type=F32)
            )
        at = pl.ds(pl.multiple_of(s * 16, 16), 16)
        prod[0, at, :] = jnp.concatenate(fwd, axis=0)
        prod[1, at, :] = jnp.concatenate(bwd, axis=0)

    lane = lax.broadcasted_iota(jnp.int32, (8, 256), 1) % 128
    row_key = jnp.full((8, 256), -1, jnp.int32)
    col_key = jnp.full((8, 256), -1, jnp.int32)
    for t in range(kt):
        mine = lane // 4 == t
        row_key = jnp.where(mine, row_of(t) * 4 + lane % 4, row_key)
        col_key = jnp.where(mine, col_of(t) * 4 + lane % 4, col_key)

    def place(key, which, pieces, out):
        p = prod[which]
        high = p.astype(BF16)
        low = (p - high.astype(F32)).astype(BF16)
        both = jnp.concatenate([high, low], axis=0)
        key = jnp.concatenate([key] * 16, axis=0)
        base = lax.broadcasted_iota(jnp.int32, (128, 256), 0)

        @pl.loop(0, pieces // 4)
        def _(s):
            pick = jnp.where(base + s * 128 == key, 1.0, 0.0).astype(BF16)
            placed = lax.dot_general(pick, both, (((1,), (0,)), ((), ())), preferred_element_type=F32)
            out[pl.ds(s * 4, 4)] = placed.reshape(4, 32, 128)

    place(col_key, 1, n_row, row_send)

    @pl.loop(1, n_row)
    def _(d):
        to = lax.rem(r + d, n_row)
        rcopy(row_send.at[to], row_recv.at[d - 1], 3, (to, c)).start()

    place(row_key, 0, n_col, col_send)

    @pl.loop(1, n_col)
    def _(d):
        to = lax.rem(c + d, n_col)
        rcopy(col_send.at[to], col_recv.at[d - 1], 4, (r, to)).start()

    drain(e1.at[pl.ds(0, n_y - 1)], 2)
    part = e1[0]
    for i in range(1, n_y):
        part = part + e1[i]
    e2[q] = part

    @pl.loop(1, 4)
    def _(d):
        rcopy(e2.at[q], e2.at[q], 5, (y * 4 + lax.rem(q + d, 4), c)).start()

    drain(e2.at[pl.ds(0, 3)], 5)
    part = e2[0]
    for i in range(1, 4):
        part = part + e2[i]
    e3[c] = part

    @pl.loop(1, n_col)
    def _(d):
        rcopy(e3.at[c], e3.at[c], 6, (r, lax.rem(c + d, n_col))).start()

    drain(e3.at[pl.ds(0, n_col - 1)], 6)
    part = e3[0]
    for i in range(1, n_col):
        part = part + e3[i]
    late[0] = part

    @pl.loop(1, n_y)
    def _(d):
        rcopy(late.at[0], late.at[1 + y], 7, (lax.rem(y + d, n_y) * 4 + q, c)).start()

    late[1 + y] = part

    drain(row_recv, 3)
    drain(col_recv, 4)
    acc = row_send[r] + col_send[c]
    for i in range(n_row - 1):
        acc = acc + row_recv[i]
    for i in range(n_col - 1):
        acc = acc + col_recv[i]
    for j in range(8):
        image[n_old:n_all, 128 * j : 128 * (j + 1)] = acc[n_vec * j : n_vec * (j + 1), :]
    fresh = image[n_all - 8 : n_all, :]
    a1[r] = jnp.zeros((8, 128), F32)
    a1[r, :, 0:n_all] = dot_nt(fresh, basis[...])

    @pl.loop(1, n_row)
    def _(d):
        rcopy(a1.at[r], a1.at[r], 8, (lax.rem(r + d, n_row), c)).start()

    drain(late.at[pl.ds(1, n_y - 1)], 7)
    scale = 1.0 / total_cols
    g = jnp.concatenate([late[1 + i] for i in range(n_all // 8)], axis=0) * scale
    inverse = lower_inverse(g[:, 0:n_all])
    old_coupling = g[:, n_all : 2 * n_all]

    drain(a1.at[pl.ds(0, n_row - 1)], 8)
    part = a1[0]
    for i in range(1, n_row):
        part = part + a1[i]
    a2[c] = part

    @pl.loop(1, n_col)
    def _(d):
        rcopy(a2.at[c], a2.at[c], 9, (r, lax.rem(c + d, n_col))).start()

    new_basis[...] = dot_nn(inverse, basis[...])
    out_basis = pltpu.make_async_copy(new_basis, basis_o, loc.at[0])
    out_basis.start()
    new_image[...] = dot_nn(inverse, image[...])
    out_image = pltpu.make_async_copy(new_image, image_o, loc.at[1])
    out_image.start()
    half = dot_nn(inverse, old_coupling)

    drain(a2.at[pl.ds(0, n_col - 1)], 9)
    part = a2[0]
    for i in range(1, n_col):
        part = part + a2[i]
    fresh = part[:, 0:n_all] * scale
    pick = lax.broadcasted_iota(jnp.int32, (8, n_all), 0) + (n_all - 8)
    spot = jnp.where(
        (pick == lax.broadcasted_iota(jnp.int32, (8, n_all), 1)) & (pick >= n_old), 1.0, 0.0
    ).astype(F32)
    fresh = lax.dot_general(fresh, spot, (((0,), (0,)), ((), ())), precision=HIGHEST, preferred_element_type=F32)
    half = half + dot_nn(inverse, fresh)
    proj[...] = dot_nt(half, inverse)
    out_proj = pltpu.make_async_copy(proj, proj_o, loc.at[2])
    out_proj.start()
    out_proj.wait()
    out_basis.wait()
    out_image.wait()


def local(tile_blocks, tile_rows, tile_cols, trial_vectors, basis_old, image_old):
    n_row = lax.axis_size("row")
    n_col = lax.axis_size("col")
    kt, ts, _ = tile_blocks.shape
    n_vec, width = trial_vectors.shape
    n_old = basis_old.shape[0]
    n_all = n_old + n_vec
    n_y = n_row // 4
    any_spec = pl.BlockSpec(memory_space=pl.ANY)
    smem = pl.BlockSpec(memory_space=pltpu.SMEM)
    v = pltpu.VMEM
    return pl.pallas_call(
        functools.partial(kernel, n_row, n_col, float(width * n_row * n_col)),
        out_shape=(
            jax.ShapeDtypeStruct((n_all, n_all), F32),
            jax.ShapeDtypeStruct((n_all, width), F32),
            jax.ShapeDtypeStruct((n_all, width), F32),
        ),
        in_specs=[smem, smem, any_spec, any_spec, any_spec, any_spec],
        out_specs=(any_spec, any_spec, any_spec),
        scratch_shapes=[
            v((kt, ts, ts), BF16),
            v((n_vec, width), BF16),
            v((n_old, width), F32),
            v((n_old, width), F32),
            v((n_all, width), F32),
            v((n_all, width), F32),
            v((2 * n_all, width), F32),
            v((8 * n_row, n_vec, ts), BF16),
            v((8 * n_col, n_vec, ts), BF16),
            v((2, 128, ts), F32),
            v((n_row, 32, ts), F32),
            v((n_col, 32, ts), F32),
            v((n_row - 1, 32, ts), F32),
            v((n_col - 1, 32, ts), F32),
            v((n_y, 8, 128), F32),
            v((n_y, 8, 128), F32),
            v((4, 8, 128), F32),
            v((n_col, 8, 128), F32),
            v((n_y + 1, 8, 128), F32),
            v((n_row, 8, 128), F32),
            v((n_col, 8, 128), F32),
            v((n_all, width), F32),
            v((n_all, width), F32),
            v((n_all, n_all), F32),
            pltpu.SemaphoreType.DMA((4,)),
            pltpu.SemaphoreType.DMA((10, 2)),
        ],
        compiler_params=pltpu.CompilerParams(
            collective_id=0, has_side_effects=True, vmem_limit_bytes=32 << 20
        ),
    )(tile_rows, tile_cols, tile_blocks, trial_vectors, basis_old, image_old)


def solution(mesh):
    in_specs = (
        P(("row", "col"), None, None),
        P(("row", "col")),
        P(("row", "col")),
        P(None, ("col", "row")),
        P(None, ("col", "row")),
        P(None, ("col", "row")),
    )
    out_specs = (P(), P(None, ("col", "row")), P(None, ("col", "row")))
    return jax.shard_map(local, mesh=mesh, in_specs=in_specs, out_specs=out_specs, check_vma=False)
```

time: 1800 us -> 67.9 us (0.04)
  waiting for transfers between devices: 1650 us -> 0 us
  blocking collectives: 102 us -> 0 us
  Pallas kernels: 0 us -> 60 us
    all_gather x1 -> x0, waiting for transfers between devices: 1390 us -> none  [local(): gathered = lax.all_gather(trial_vectors, ('row', 'col'), axis=1, tiled=True)]
    reduce_scatter x1 -> x0, waiting for transfers between devices: 129 us -> none  [local(): lax.psum_scatter(col_partial, 'row', scatter_dimension=0, tiled=True)]
    psum x1 -> x0, waiting for transfers between devices: 129 us -> none  [local(): row_total = lax.psum(row_partial, 'col')]
    psum x1 -> x0, blocking collectives: 102 us -> none  [local(): lax.psum((rows_product(basis_all, basis_all), rows_product(basis_all, ima...]
    pallas_call x0 -> x1, Pallas kernels: none -> 60 us  [local(): pl.pallas_call(functools.partial(kernel, n_row, n_col, float(width * n_ro...]
  transfers between devices with their start and end apart: 3 -> 0, of which waited for: 3 -> 0; matrix products, arithmetic and copies ran while one was open for 0% -> 0% of each run, Pallas kernels for 0% -> 0%
where the time goes in v1:
time: 67.9 us; the launch traced here: 67.6 us
  Pallas kernels  60 us (88%)
  local copies, waits for them, and re-layouts  6.95 us (10%)
    pallas_call x1, Pallas kernels, local(): pl.pallas_call(functools.partial(kernel, n_row, n_col, float(width * n_ro...  60 us
    unnamed x15, local copies, waits for them, and re-layouts  6.95 us

profile of v1, /device:TPU:1, one launch (start us, length us, event | category | flops | bytes accessed | tf_op | source)
XLA Modules:
  0.0 67.6 jit_solution(3825759898223479090)
XLA Ops:
  0.6 0.0 copy-start
  0.6 1.1 %copy-done = bf16[24,128,128]{2,1,0:T(8,128)(2,1)S(1)} copy-done((bf16[24,128,128]{2,1,0:T(8,128)(2,1)S(1)}, bf16[24,128,128]{2,1,0:T(8,128)(2,1)}, u32[]{:S(2)}) %copy-start) | copy-done | bytes 786456
  1.8 0.0 copy-start.1
  1.8 0.9 %copy-done.1 = f32[44,1024]{1,0:T(8,128)S(1)} copy-done((f32[44,1024]{1,0:T(8,128)S(1)}, f32[44,1024]{1,0:T(8,128)}, u32[]{:S(2)}) %copy-start.1) | copy-done | bytes 180248
  2.7 0.0 copy-start.2
  2.7 0.9 %copy-done.2 = f32[44,1024]{1,0:T(8,128)S(1)} copy-done((f32[44,1024]{1,0:T(8,128)S(1)}, f32[44,1024]{1,0:T(8,128)}, u32[]{:S(2)}) %copy-start.2) | copy-done | bytes 180248
  3.6 0.0 copy-start.3
  3.6 0.7 %copy-done.3 = bf16[4,1024]{1,0:T(4,128)(2,1)S(1)} copy-done((bf16[4,1024]{1,0:T(4,128)(2,1)S(1)}, bf16[4,1024]{1,0:T(4,128)(2,1)}, u32[]{:S(2)}) %copy-start.3) | copy-done | bytes 8216
  4.3 0.0 copy-start.4
  4.3 0.7 copy-done.4
  5.0 0.0 copy-start.5
  5.0 0.7 copy-done.5
  5.6 60.0 %shard_map.85 = (f32[48,48]{1,0:T(8,128)S(1)}, f32[48,1024]{1,0:T(8,128)S(1)}, f32[48,1024]{1,0:T(8,128)S(1)}) custom-call(s32[24]{0:T(128)S(1)} %copy-done.4, s32[24]{0:T(128)S(1)} %copy-done.5, bf16[24,128,128]{2,1,0:T(8,128)(2,1)S(1)} %copy-done, bf16[4,1024]{1,0:T(4,128)(2,1)S(1)} %copy-done.3, f32[44,1024]{1,0:T(8,128)S(1)} %copy-done.1, ...), custom_call_target="tpu_custom_call" | custom-call | tf_op jit(solution)/shard_map/pallas_call | solution.py:303
  65.7 0.6 copy.12
  66.3 0.7 %copy.13 = f32[48,1024]{1,0:T(8,128)} copy(f32[48,1024]{1,0:T(8,128)S(1)} %get-tuple-element.7) | data formatting | bytes 393216
  66.9 0.7 %copy.14 = f32[48,1024]{1,0:T(8,128)} copy(f32[48,1024]{1,0:T(8,128)S(1)} %get-tuple-element.8) | data formatting | bytes 393216
Async XLA Ops:
  0.6 1.1 %copy-start = (bf16[24,128,128]{2,1,0:T(8,128)(2,1)S(1)}, bf16[24,128,128]{2,1,0:T(8,128)(2,1)}, u32[]{:S(2)}) copy-start(bf16[24,128,128]{2,1,0:T(8,128)(2,1)} %tiles_h.1) | copy-start | bytes 2359300
  1.8 0.9 %copy-start.1 = (f32[44,1024]{1,0:T(8,128)S(1)}, f32[44,1024]{1,0:T(8,128)}, u32[]{:S(2)}) copy-start(f32[44,1024]{1,0:T(8,128)} %basis_h.1) | copy-start | bytes 540676
  2.7 0.9 %copy-start.2 = (f32[44,1024]{1,0:T(8,128)S(1)}, f32[44,1024]{1,0:T(8,128)}, u32[]{:S(2)}) copy-start(f32[44,1024]{1,0:T(8,128)} %image_h.1) | copy-start | bytes 540676
  3.6 0.7 %copy-start.3 = (bf16[4,1024]{1,0:T(4,128)(2,1)S(1)}, bf16[4,1024]{1,0:T(4,128)(2,1)}, u32[]{:S(2)}) copy-start(bf16[4,1024]{1,0:T(4,128)(2,1)} %trial_h.1) | copy-start | bytes 24580
  4.3 0.7 copy-start.4
  5.0 0.7 copy-start.5

commit v2 on v1

--- a/solution.py
+++ b/solution.py
@@ -50,10 +50,10 @@
 
 def kernel(
     n_row, n_col, total_cols,
-    rows_s, cols_s, tiles_h, trial_h, basis_h, image_h,
+    rows_h, cols_h, tiles_h, trial_h, basis_h, image_h,
     proj_o, basis_o, image_o,
-    tiles, trial, old_basis, old_image, basis, image, mix,
-    x_row, x_col, prod, row_send, col_send, row_recv, col_recv,
+    rows_s, cols_s, tiles, trial, old_basis, old_image, basis, image, mix,
+    x_row, x_col, prod, prod2, keys, row_send, col_send, row_recv, col_recv,
     gram, e1, e2, e3, late, a1, a2, new_basis, new_image, proj,
     loc, sem,
 ):
@@ -71,6 +71,8 @@
         pltpu.make_async_copy(basis_h, old_basis, loc.at[1]),
         pltpu.make_async_copy(image_h, old_image, loc.at[2]),
         pltpu.make_async_copy(tiles_h, tiles, loc.at[3]),
+        pltpu.make_async_copy(rows_h, rows_s, loc.at[4]),
+        pltpu.make_async_copy(cols_h, cols_s, loc.at[5]),
     ]
     for copy in local:
         copy.start()
@@ -102,15 +104,40 @@
         w.wait_send()
         w.wait_recv()
 
-    @pl.loop(1, n_row)
-    def _(d):
+    def far_first(i, n):
+        return lax.rem(n // 2 + (i + 1) // 2 * (1 - i % 2 * 2) + n, n)
+
+    @pl.loop(0, n_col - 1)
+    def _(i):
+        own = pl.ds(c * 8, 8)
+        rcopy(x_col.at[own], x_col.at[own], 1, (r, lax.rem(c + far_first(i, n_col), n_col))).start()
+
+    @pl.loop(0, n_row - 1)
+    def _(i):
         own = pl.ds(r * 8, 8)
-        rcopy(x_row.at[own], x_row.at[own], 0, (lax.rem(r + d, n_row), c)).start()
-
-    @pl.loop(1, n_col)
-    def _(d):
-        own = pl.ds(c * 8, 8)
-        rcopy(x_col.at[own], x_col.at[own], 1, (r, lax.rem(c + d, n_col))).start()
+        rcopy(x_row.at[own], x_row.at[own], 0, (lax.rem(r + far_first(i, n_row), n_row), c)).start()
+
+    local[4].wait()
+    local[5].wait()
+
+    def row_of(t):
+        b = rows_s[t]
+        return b // (8 * n_row) * 8 + b % 8
+
+    def col_of(t):
+        return cols_s[t] % (8 * n_row)
+
+    lane = lax.broadcasted_iota(jnp.int32, (8, 128), 1)
+    row_key = jnp.full((8, 128), -1, jnp.int32)
+    col_key = jnp.full((8, 128), -1, jnp.int32)
+    for t in range(kt):
+        mine = lane // 4 == t
+        row_key = jnp.where(mine, row_of(t) * 4 + lane % 4, row_key)
+        col_key = jnp.where(mine, col_of(t) * 4 + lane % 4, col_key)
+    keys[0] = col_key
+    core = r % 2
+    twin = (r + 1 - 2 * core, c)
+    rcopy(keys.at[0], keys.at[1], 10, twin).start()
 
     local[1].wait()
     local[2].wait()
@@ -133,67 +160,66 @@
         rcopy(gram.at[to], e1.at[y], 2, (to * 4 + q, c)).start()
 
     local[3].wait()
+    prod[...] = jnp.zeros(prod.shape, F32)
+
+    def products(which, x, index, along):
+        @pl.loop(0, kt // 4)
+        def _(s):
+            out = []
+            for u in range(4):
+                t = s * 4 + u
+                out.append(
+                    lax.dot_general(
+                        x[index(t)], tiles[t], (((1,), (along,)), ((), ())), preferred_element_type=F32)
+                )
+            prod[which, pl.ds(pl.multiple_of(s * 16, 16), 16), :] = jnp.concatenate(out, axis=0)
+
+    def split(p):
+        high = p.astype(BF16)
+        return high, (p - high.astype(F32)).astype(BF16)
+
+    drain(x_col.at[pl.ds(0, (n_col - 1) * 8)], 1)
+    products(1, x_col, row_of, 0)
+    rcopy(prod.at[1], prod2, 11, twin).start()
+
     drain(x_row.at[pl.ds(0, (n_row - 1) * 8)], 0)
-    drain(x_col.at[pl.ds(0, (n_col - 1) * 8)], 1)
-
-    def row_of(t):
-        b = rows_s[t]
-        return b // (8 * n_row) * 8 + b % 8
-
-    def col_of(t):
-        return cols_s[t] % (8 * n_row)
-
-    prod[...] = jnp.zeros(prod.shape, F32)
-
-    @pl.loop(0, kt // 4)
+    products(0, x_row, col_of, 1)
+
+    drain(keys.at[1], 10)
+    drain(prod2, 11)
+    both = jnp.concatenate([*split(prod[1]), *split(prod2[...])], axis=0)
+    key = jnp.concatenate([jnp.concatenate([keys[0]] * 2 + [keys[1]] * 2, axis=1)] * 16, axis=0)
+    at = lax.broadcasted_iota(jnp.int32, (128, 512), 0)
+    at = (at // 32 * 2 + core) * 32 + at % 32
+
+    @pl.loop(0, n_row // 8)
     def _(s):
-        fwd, bwd = [], []
-        for u in range(4):
-            t = s * 4 + u
-            tile = tiles[t]
-            fwd.append(
-                lax.dot_general(x_row[col_of(t)], tile, (((1,), (1,)), ((), ())), preferred_element_type=F32)
-            )
-            bwd.append(
-                lax.dot_general(x_col[row_of(t)], tile, (((1,), (0,)), ((), ())), preferred_element_type=F32)
-            )
-        at = pl.ds(pl.multiple_of(s * 16, 16), 16)
-        prod[0, at, :] = jnp.concatenate(fwd, axis=0)
-        prod[1, at, :] = jnp.concatenate(bwd, axis=0)
-
-    lane = lax.broadcasted_iota(jnp.int32, (8, 256), 1) % 128
-    row_key = jnp.full((8, 256), -1, jnp.int32)
-    col_key = jnp.full((8, 256), -1, jnp.int32)
-    for t in range(kt):
-        mine = lane // 4 == t
-        row_key = jnp.where(mine, row_of(t) * 4 + lane % 4, row_key)
-        col_key = jnp.where(mine, col_of(t) * 4 + lane % 4, col_key)
-
-    def place(key, which, pieces, out):
-        p = prod[which]
-        high = p.astype(BF16)
-        low = (p - high.astype(F32)).astype(BF16)
-        both = jnp.concatenate([high, low], axis=0)
-        key = jnp.concatenate([key] * 16, axis=0)
-        base = lax.broadcasted_iota(jnp.int32, (128, 256), 0)
-
-        @pl.loop(0, pieces // 4)
-        def _(s):
-            pick = jnp.where(base + s * 128 == key, 1.0, 0.0).astype(BF16)
-            placed = lax.dot_general(pick, both, (((1,), (0,)), ((), ())), preferred_element_type=F32)
-            out[pl.ds(s * 4, 4)] = placed.reshape(4, 32, 128)
-
-    place(col_key, 1, n_row, row_send)
-
-    @pl.loop(1, n_row)
-    def _(d):
-        to = lax.rem(r + d, n_row)
-        rcopy(row_send.at[to], row_recv.at[d - 1], 3, (to, c)).start()
-
-    place(row_key, 0, n_col, col_send)
-
-    @pl.loop(1, n_col)
-    def _(d):
+        pick = jnp.where(at + s * 256 == key, 1.0, 0.0).astype(BF16)
+        placed = lax.dot_general(pick, both, (((1,), (0,)), ((), ())), preferred_element_type=F32)
+        row_send[pl.ds(s * 4, 4)] = placed.reshape(4, 32, 128)
+
+    half = n_row // 2
+    pair = r // 2
+
+    @pl.loop(0, half - 1)
+    def _(i):
+        d = far_first(i, half)
+        to = lax.rem(pair + d, half)
+        rcopy(row_send.at[to], row_recv.at[d - 1], 3, (to * 2 + core, c)).start()
+
+    both = jnp.concatenate(split(prod[0]), axis=0)
+    key = jnp.concatenate([jnp.concatenate([row_key] * 2, axis=1)] * 16, axis=0)
+    at = lax.broadcasted_iota(jnp.int32, (128, 256), 0)
+
+    @pl.loop(0, n_col // 4)
+    def _(s):
+        pick = jnp.where(at + s * 128 == key, 1.0, 0.0).astype(BF16)
+        placed = lax.dot_general(pick, both, (((1,), (0,)), ((), ())), preferred_element_type=F32)
+        col_send[pl.ds(s * 4, 4)] = placed.reshape(4, 32, 128)
+
+    @pl.loop(0, n_col - 1)
+    def _(i):
+        d = far_first(i, n_col)
         to = lax.rem(c + d, n_col)
         rcopy(col_send.at[to], col_recv.at[d - 1], 4, (r, to)).start()
 
@@ -231,8 +257,8 @@
 
     drain(row_recv, 3)
     drain(col_recv, 4)
-    acc = row_send[r] + col_send[c]
-    for i in range(n_row - 1):
+    acc = row_send[pair] + col_send[c]
+    for i in range(half - 1):
         acc = acc + row_recv[i]
     for i in range(n_col - 1):
         acc = acc + col_recv[i]
@@ -268,20 +294,16 @@
     new_image[...] = dot_nn(inverse, image[...])
     out_image = pltpu.make_async_copy(new_image, image_o, loc.at[1])
     out_image.start()
-    half = dot_nn(inverse, old_coupling)
+    base = dot_nt(dot_nn(inverse, old_coupling), inverse)
+    last = jnp.swapaxes(inverse[:, n_all - 8 : n_all], 0, 1)
+    last = jnp.where(lax.broadcasted_iota(jnp.int32, (8, n_all), 0) >= 8 - n_vec, last, 0.0)
 
     drain(a2.at[pl.ds(0, n_col - 1)], 9)
     part = a2[0]
     for i in range(1, n_col):
         part = part + a2[i]
     fresh = part[:, 0:n_all] * scale
-    pick = lax.broadcasted_iota(jnp.int32, (8, n_all), 0) + (n_all - 8)
-    spot = jnp.where(
-        (pick == lax.broadcasted_iota(jnp.int32, (8, n_all), 1)) & (pick >= n_old), 1.0, 0.0
-    ).astype(F32)
-    fresh = lax.dot_general(fresh, spot, (((0,), (0,)), ((), ())), precision=HIGHEST, preferred_element_type=F32)
-    half = half + dot_nn(inverse, fresh)
-    proj[...] = dot_nt(half, inverse)
+    proj[...] = base + dot_nn(dot_nt(inverse, fresh), last)
     out_proj = pltpu.make_async_copy(proj, proj_o, loc.at[2])
     out_proj.start()
     out_proj.wait()
@@ -297,8 +319,7 @@
     n_old = basis_old.shape[0]
     n_all = n_old + n_vec
     n_y = n_row // 4
-    any_spec = pl.BlockSpec(memory_space=pl.ANY)
-    smem = pl.BlockSpec(memory_space=pltpu.SMEM)
+    hbm = pl.BlockSpec(memory_space=pltpu.HBM)
     v = pltpu.VMEM
     return pl.pallas_call(
         functools.partial(kernel, n_row, n_col, float(width * n_row * n_col)),
@@ -307,9 +328,11 @@
             jax.ShapeDtypeStruct((n_all, width), F32),
             jax.ShapeDtypeStruct((n_all, width), F32),
         ),
-        in_specs=[smem, smem, any_spec, any_spec, any_spec, any_spec],
-        out_specs=(any_spec, any_spec, any_spec),
+        in_specs=[hbm] * 6,
+        out_specs=(hbm, hbm, hbm),
         scratch_shapes=[
+            pltpu.SMEM((kt,), jnp.int32),
+            pltpu.SMEM((kt,), jnp.int32),
             v((kt, ts, ts), BF16),
             v((n_vec, width), BF16),
             v((n_old, width), F32),
@@ -320,9 +343,11 @@
             v((8 * n_row, n_vec, ts), BF16),
             v((8 * n_col, n_vec, ts), BF16),
             v((2, 128, ts), F32),
-            v((n_row, 32, ts), F32),
+            v((128, ts), F32),
+            v((2, 8, 128), jnp.int32),
+            v((n_row // 2, 32, ts), F32),
             v((n_col, 32, ts), F32),
-            v((n_row - 1, 32, ts), F32),
+            v((n_row // 2 - 1, 32, ts), F32),
             v((n_col - 1, 32, ts), F32),
             v((n_y, 8, 128), F32),
             v((n_y, 8, 128), F32),
@@ -334,11 +359,11 @@
             v((n_all, width), F32),
             v((n_all, width), F32),
             v((n_all, n_all), F32),
-            pltpu.SemaphoreType.DMA((4,)),
-            pltpu.SemaphoreType.DMA((10, 2)),
+            pltpu.SemaphoreType.DMA((6,)),
+            pltpu.SemaphoreType.DMA((12, 2)),
         ],
         compiler_params=pltpu.CompilerParams(
-            collective_id=0, has_side_effects=True, vmem_limit_bytes=32 << 20
+            collective_id=0, has_side_effects=True, vmem_limit_bytes=60 << 20
         ),
     )(tile_rows, tile_cols, tile_blocks, trial_vectors, basis_old, image_old)
 

time: 67.9 us -> 60.5 us (0.89); the launches traced: 67.6 us -> 59.4 us
  Pallas kernels: 60 us -> 55.1 us
  local copies, waits for them, and re-layouts: 6.95 us -> 3.68 us
    pallas_call x1, Pallas kernels: 60 us -> 55.1 us  [local(): pl.pallas_call(functools.partial(kernel, n_row, n_col, float(width * n_ro...]
    unnamed x15 -> x5, local copies, waits for them, and re-layouts: 6.95 us -> 3.68 us
where the time goes in v2:
time: 60.5 us; the launch traced here: 59.4 us
  Pallas kernels  55.1 us (91%)
  local copies, waits for them, and re-layouts  3.68 us (6%)
  between operations  0.64 us (1%)
    pallas_call x1, Pallas kernels, local(): pl.pallas_call(functools.partial(kernel, n_row, n_col, float(width * n_ro...  55.1 us
    unnamed x5, local copies, waits for them, and re-layouts  3.68 us

profile of v2, /device:TPU:1, one launch (start us, length us, event | category | flops | bytes accessed | tf_op | source)
XLA Modules:
  0.0 59.4 jit_solution(16254769791212555982)
XLA Ops:
  0.6 55.1 %shard_map.85 = (f32[48,48]{1,0:T(8,128)}, f32[48,1024]{1,0:T(8,128)}, f32[48,1024]{1,0:T(8,128)}) custom-call(s32[24]{0:T(128)} %rows_h.1, s32[24]{0:T(128)} %cols_h.1, bf16[24,128,128]{2,1,0:T(8,128)(2,1)} %tiles_h.1, bf16[4,1024]{1,0:T(4,128)(2,1)} %trial_h.1, f32[44,1024]{1,0:T(8,128)} %basis_h.1, f32[44,1024]{1,0:T(8,128)} %image_h.1), custom_call_target="tpu_custom_call" | custom-call | tf_op jit(solution)/shard_map/pallas_call | solution.py:324
  55.7 1.3 %copy.12 = f32[48,48]{1,0:T(8,128)} copy(f32[48,48]{1,0:T(8,128)} %get-tuple-element.6) | data formatting | bytes 18432
  57.0 0.0 copy-start
  57.1 1.7 %copy.13 = f32[48,1024]{1,0:T(8,128)} copy(f32[48,1024]{1,0:T(8,128)} %get-tuple-element.7) | data formatting | bytes 393216
  58.7 0.0 copy-done
  58.7 0.7 %copy.14 = f32[48,1024]{1,0:T(8,128)} copy(f32[48,1024]{1,0:T(8,128)S(1)} %copy-done) | data formatting | bytes 393216
Async XLA Ops:
  57.0 1.7 %copy-start = (f32[48,1024]{1,0:T(8,128)S(1)}, f32[48,1024]{1,0:T(8,128)}, u32[]{:S(2)}) copy-start(f32[48,1024]{1,0:T(8,128)} %get-tuple-element.8) | copy-start | bytes 589828

commit v3 on v2

--- a/solution.py
+++ b/solution.py
@@ -54,7 +54,7 @@
     proj_o, basis_o, image_o,
     rows_s, cols_s, tiles, trial, old_basis, old_image, basis, image, mix,
     x_row, x_col, prod, prod2, keys, row_send, col_send, row_recv, col_recv,
-    gram, e1, e2, e3, late, a1, a2, new_basis, new_image, proj,
+    gram, e1, e2, sums, a1, a2, new_basis, new_image, proj,
     loc, sem,
 ):
     r = lax.axis_index("row")
@@ -63,8 +63,10 @@
     n_vec = trial_h.shape[0]
     n_all = n_old + n_vec
     kt = tiles.shape[0]
-    n_y = n_row // 4
-    y, q = r // 4, r % 4
+    pieces = n_all // 8
+    step = n_row // pieces
+    piece = r // step
+    owner = (r % step == 0) & (piece < pieces)
 
     local = [
         pltpu.make_async_copy(trial_h, trial, loc.at[0]),
@@ -152,12 +154,11 @@
     for i in range(n_all // 8):
         gram[i, :, 0 : 2 * n_all] = g[8 * i : 8 * i + 8, :]
 
-    e1[y] = gram[y]
-
-    @pl.loop(1, n_y)
-    def _(d):
-        to = lax.rem(y + d, n_y)
-        rcopy(gram.at[to], e1.at[y], 2, (to * 4 + q, c)).start()
+    @pl.loop(0, pieces)
+    def _(p):
+        @pl.when(p * step != r)
+        def _():
+            rcopy(gram.at[p], e1.at[r], 2, (p * step, c)).start()
 
     local[3].wait()
     prod[...] = jnp.zeros(prod.shape, F32)
@@ -182,6 +183,25 @@
     products(1, x_col, row_of, 0)
     rcopy(prod.at[1], prod2, 11, twin).start()
 
+    @pl.when(owner)
+    def _():
+        rcopy(e1.at[pl.ds(0, n_row - 1)], e1.at[pl.ds(0, n_row - 1)], 2, (r, c)).wait_recv()
+        gone = gram.at[pl.ds(0, pieces - 1)]
+        rcopy(gone, gone, 2, (r, c)).wait_send()
+        e1[r] = gram[piece]
+        part = e1[0]
+        for i in range(1, n_row):
+            part = part + e1[i]
+        e2[c] = part
+
+        @pl.loop(0, n_col - 1)
+        def _(i):
+            rcopy(e2.at[c], e2.at[c], 5, (r, lax.rem(c + far_first(i, n_col), n_col))).start()
+
+    @pl.when(jnp.logical_not(owner))
+    def _():
+        rcopy(gram, gram, 2, (r, c)).wait_send()
+
     drain(x_row.at[pl.ds(0, (n_row - 1) * 8)], 0)
     products(0, x_row, col_of, 1)
 
@@ -223,37 +243,18 @@
         to = lax.rem(c + d, n_col)
         rcopy(col_send.at[to], col_recv.at[d - 1], 4, (r, to)).start()
 
-    drain(e1.at[pl.ds(0, n_y - 1)], 2)
-    part = e1[0]
-    for i in range(1, n_y):
-        part = part + e1[i]
-    e2[q] = part
-
-    @pl.loop(1, 4)
-    def _(d):
-        rcopy(e2.at[q], e2.at[q], 5, (y * 4 + lax.rem(q + d, 4), c)).start()
-
-    drain(e2.at[pl.ds(0, 3)], 5)
-    part = e2[0]
-    for i in range(1, 4):
-        part = part + e2[i]
-    e3[c] = part
-
-    @pl.loop(1, n_col)
-    def _(d):
-        rcopy(e3.at[c], e3.at[c], 6, (r, lax.rem(c + d, n_col))).start()
-
-    drain(e3.at[pl.ds(0, n_col - 1)], 6)
-    part = e3[0]
-    for i in range(1, n_col):
-        part = part + e3[i]
-    late[0] = part
-
-    @pl.loop(1, n_y)
-    def _(d):
-        rcopy(late.at[0], late.at[1 + y], 7, (lax.rem(y + d, n_y) * 4 + q, c)).start()
-
-    late[1 + y] = part
+    @pl.when(owner)
+    def _():
+        drain(e2.at[pl.ds(0, n_col - 1)], 5)
+        part = e2[0]
+        for i in range(1, n_col):
+            part = part + e2[i]
+        sums[piece] = part
+
+        @pl.loop(0, n_row - 1)
+        def _(i):
+            to = lax.rem(r + far_first(i, n_row), n_row)
+            rcopy(sums.at[piece], sums.at[piece], 6, (to, c)).start()
 
     drain(row_recv, 3)
     drain(col_recv, 4)
@@ -268,13 +269,23 @@
     a1[r] = jnp.zeros((8, 128), F32)
     a1[r, :, 0:n_all] = dot_nt(fresh, basis[...])
 
-    @pl.loop(1, n_row)
-    def _(d):
-        rcopy(a1.at[r], a1.at[r], 8, (lax.rem(r + d, n_row), c)).start()
-
-    drain(late.at[pl.ds(1, n_y - 1)], 7)
+    @pl.loop(0, n_row - 1)
+    def _(i):
+        rcopy(a1.at[r], a1.at[r], 8, (lax.rem(r + far_first(i, n_row), n_row), c)).start()
+
+    @pl.when(owner)
+    def _():
+        came = sums.at[pl.ds(0, pieces - 1)]
+        rcopy(came, came, 6, (r, c)).wait_recv()
+        gone = e1.at[pl.ds(0, n_row - 1)]
+        rcopy(gone, gone, 6, (r, c)).wait_send()
+
+    @pl.when(jnp.logical_not(owner))
+    def _():
+        rcopy(sums, sums, 6, (r, c)).wait_recv()
+
     scale = 1.0 / total_cols
-    g = jnp.concatenate([late[1 + i] for i in range(n_all // 8)], axis=0) * scale
+    g = jnp.concatenate([sums[i] for i in range(pieces)], axis=0) * scale
     inverse = lower_inverse(g[:, 0:n_all])
     old_coupling = g[:, n_all : 2 * n_all]
 
@@ -284,9 +295,9 @@
         part = part + a1[i]
     a2[c] = part
 
-    @pl.loop(1, n_col)
-    def _(d):
-        rcopy(a2.at[c], a2.at[c], 9, (r, lax.rem(c + d, n_col))).start()
+    @pl.loop(0, n_col - 1)
+    def _(i):
+        rcopy(a2.at[c], a2.at[c], 9, (r, lax.rem(c + far_first(i, n_col), n_col))).start()
 
     new_basis[...] = dot_nn(inverse, basis[...])
     out_basis = pltpu.make_async_copy(new_basis, basis_o, loc.at[0])
@@ -311,6 +322,18 @@
     out_image.wait()
 
 
+def hand_out(a_in, b_in, c_in, a_out, b_out, c_out, a, b, c, sem):
+    loads = [pltpu.make_async_copy(x, y, sem.at[i]) for i, (x, y) in enumerate(((a_in, a), (b_in, b), (c_in, c)))]
+    stores = [pltpu.make_async_copy(x, y, sem.at[3 + i]) for i, (x, y) in enumerate(((a, a_out), (b, b_out), (c, c_out)))]
+    for copy in loads:
+        copy.start()
+    for load, store in zip(loads, stores):
+        load.wait()
+        store.start()
+    for copy in stores:
+        copy.wait()
+
+
 def local(tile_blocks, tile_rows, tile_cols, trial_vectors, basis_old, image_old):
     n_row = lax.axis_size("row")
     n_col = lax.axis_size("col")
@@ -318,10 +341,9 @@
     n_vec, width = trial_vectors.shape
     n_old = basis_old.shape[0]
     n_all = n_old + n_vec
-    n_y = n_row // 4
     hbm = pl.BlockSpec(memory_space=pltpu.HBM)
     v = pltpu.VMEM
-    return pl.pallas_call(
+    outs = pl.pallas_call(
         functools.partial(kernel, n_row, n_col, float(width * n_row * n_col)),
         out_shape=(
             jax.ShapeDtypeStruct((n_all, n_all), F32),
@@ -349,11 +371,10 @@
             v((n_col, 32, ts), F32),
             v((n_row // 2 - 1, 32, ts), F32),
             v((n_col - 1, 32, ts), F32),
-            v((n_y, 8, 128), F32),
-            v((n_y, 8, 128), F32),
-            v((4, 8, 128), F32),
+            v((n_all // 8, 8, 128), F32),
+            v((n_row, 8, 128), F32),
             v((n_col, 8, 128), F32),
-            v((n_y + 1, 8, 128), F32),
+            v((n_all // 8, 8, 128), F32),
             v((n_row, 8, 128), F32),
             v((n_col, 8, 128), F32),
             v((n_all, width), F32),
@@ -366,6 +387,14 @@
             collective_id=0, has_side_effects=True, vmem_limit_bytes=60 << 20
         ),
     )(tile_rows, tile_cols, tile_blocks, trial_vectors, basis_old, image_old)
+    return pl.pallas_call(
+        hand_out,
+        out_shape=tuple(jax.ShapeDtypeStruct(o.shape, o.dtype) for o in outs),
+        in_specs=[hbm] * 3,
+        out_specs=(hbm,) * 3,
+        scratch_shapes=[v(o.shape, o.dtype) for o in outs] + [pltpu.SemaphoreType.DMA((6,))],
+        compiler_params=pltpu.CompilerParams(vmem_limit_bytes=60 << 20),
+    )(*outs)
 
 
 def solution(mesh):

time: 60.5 us -> 52 us (0.86); the launches traced: 59.4 us -> 51.8 us
  Pallas kernels: 55.1 us -> 51.2 us
  local copies, waits for them, and re-layouts: 3.68 us -> 0 us
    pallas_call x1, Pallas kernels: 55.1 us -> 49.4 us  [local(): pl.pallas_call(functools.partial(kernel, n_row, n_col, float(width * n_ro...]
    unnamed x5 -> x0, local copies, waits for them, and re-layouts: 3.68 us -> none
    pallas_call x0 -> x1, Pallas kernels: none -> 1.77 us  [local(): pl.pallas_call(hand_out, out_shape=tuple((jax.ShapeDtypeStruct(o.shape, o...]
where the time goes in v3:
time: 52 us; the launch traced here: 51.8 us
  Pallas kernels  51.2 us (98%)
  between operations  0.64 us (1%)
    pallas_call x1, Pallas kernels, local(): pl.pallas_call(functools.partial(kernel, n_row, n_col, float(width * n_ro...  49.4 us
    pallas_call x1, Pallas kernels, local(): pl.pallas_call(hand_out, out_shape=tuple((jax.ShapeDtypeStruct(o.shape, o...  1.77 us

profile of v3, /device:TPU:1, one launch (start us, length us, event | category | flops | bytes accessed | tf_op | source)
XLA Modules:
  0.0 51.8 jit_solution(10665099632097458064)
XLA Ops:
  0.6 49.4 %shard_map.85 = (f32[48,48]{1,0:T(8,128)}, f32[48,1024]{1,0:T(8,128)}, f32[48,1024]{1,0:T(8,128)}) custom-call(s32[24]{0:T(128)} %rows_h.1, s32[24]{0:T(128)} %cols_h.1, bf16[24,128,128]{2,1,0:T(8,128)(2,1)} %tiles_h.1, bf16[4,1024]{1,0:T(4,128)(2,1)} %trial_h.1, f32[44,1024]{1,0:T(8,128)} %basis_h.1, f32[44,1024]{1,0:T(8,128)} %image_h.1), custom_call_target="tpu_custom_call" | custom-call | tf_op jit(solution)/shard_map/pallas_call | solution.py:346
  50.1 1.8 %shard_map.86 = (f32[48,48]{1,0:T(8,128)}, f32[48,1024]{1,0:T(8,128)}, f32[48,1024]{1,0:T(8,128)}) custom-call(f32[48,48]{1,0:T(8,128)} %get-tuple-element.6.a_in, f32[48,1024]{1,0:T(8,128)} %get-tuple-element.7.b_in, f32[48,1024]{1,0:T(8,128)} %get-tuple-element.8.c_in), custom_call_target="tpu_custom_call" | custom-call | tf_op jit(solution)/shard_map/pallas_call | solution.py:390

commit v4 on v3

--- a/solution.py
+++ b/solution.py
@@ -55,7 +55,7 @@
     rows_s, cols_s, tiles, trial, old_basis, old_image, basis, image, mix,
     x_row, x_col, prod, prod2, keys, row_send, col_send, row_recv, col_recv,
     gram, e1, e2, sums, a1, a2, new_basis, new_image, proj,
-    loc, sem,
+    loc, sem, relay,
 ):
     r = lax.axis_index("row")
     c = lax.axis_index("col")
@@ -114,10 +114,21 @@
         own = pl.ds(c * 8, 8)
         rcopy(x_col.at[own], x_col.at[own], 1, (r, lax.rem(c + far_first(i, n_col), n_col))).start()
 
-    @pl.loop(0, n_row - 1)
-    def _(i):
-        own = pl.ds(r * 8, 8)
-        rcopy(x_row.at[own], x_row.at[own], 0, (lax.rem(r + far_first(i, n_row), n_row), c)).start()
+    half = n_row // 2
+    pair = r // 2
+    core = r % 2
+    twin = (r + 1 - 2 * core, c)
+    own = pl.ds(r * 8, 8)
+
+    @pl.loop(0, half - 1)
+    def _(i):
+        d = far_first(i, half)
+        to = lax.rem(pair + d, half) * 2 + core
+        pltpu.make_async_remote_copy(
+            x_row.at[own], x_row.at[own], sem.at[0, 0], relay.at[d], device_id=(to, c), device_id_type=MESH
+        ).start()
+
+    rcopy(x_row.at[own], x_row.at[own], 7, twin).start()
 
     local[4].wait()
     local[5].wait()
@@ -137,8 +148,6 @@
         row_key = jnp.where(mine, row_of(t) * 4 + lane % 4, row_key)
         col_key = jnp.where(mine, col_of(t) * 4 + lane % 4, col_key)
     keys[0] = col_key
-    core = r % 2
-    twin = (r + 1 - 2 * core, c)
     rcopy(keys.at[0], keys.at[1], 10, twin).start()
 
     local[1].wait()
@@ -202,8 +211,15 @@
     def _():
         rcopy(gram, gram, 2, (r, c)).wait_send()
 
-    drain(x_row.at[pl.ds(0, (n_row - 1) * 8)], 0)
-    products(0, x_row, col_of, 1)
+    @pl.loop(0, half - 1)
+    def _(i):
+        d = far_first(half - 2 - i, half)
+        at = pl.ds(lax.rem(pair - d + half, half) * 16 + core * 8, 8)
+        piece_in = x_row.at[at]
+        pltpu.make_async_remote_copy(
+            piece_in, piece_in, sem.at[0, 0], relay.at[d], device_id=(r, c), device_id_type=MESH
+        ).wait_recv()
+        rcopy(piece_in, piece_in, 7, twin).start()
 
     drain(keys.at[1], 10)
     drain(prod2, 11)
@@ -218,15 +234,16 @@
         placed = lax.dot_general(pick, both, (((1,), (0,)), ((), ())), preferred_element_type=F32)
         row_send[pl.ds(s * 4, 4)] = placed.reshape(4, 32, 128)
 
-    half = n_row // 2
-    pair = r // 2
-
     @pl.loop(0, half - 1)
     def _(i):
         d = far_first(i, half)
         to = lax.rem(pair + d, half)
         rcopy(row_send.at[to], row_recv.at[d - 1], 3, (to * 2 + core, c)).start()
 
+    drain(x_row.at[pl.ds(0, half * 8)], 7)
+    sent = x_row.at[pl.ds(0, (half - 1) * 8)]
+    rcopy(sent, sent, 0, (r, c)).wait_send()
+    products(0, x_row, col_of, 1)
     both = jnp.concatenate(split(prod[0]), axis=0)
     key = jnp.concatenate([jnp.concatenate([row_key] * 2, axis=1)] * 16, axis=0)
     at = lax.broadcasted_iota(jnp.int32, (128, 256), 0)
@@ -266,8 +283,10 @@
     for j in range(8):
         image[n_old:n_all, 128 * j : 128 * (j + 1)] = acc[n_vec * j : n_vec * (j + 1), :]
     fresh = image[n_all - 8 : n_all, :]
-    a1[r] = jnp.zeros((8, 128), F32)
-    a1[r, :, 0:n_all] = dot_nt(fresh, basis[...])
+    fresh = dot_nt(fresh, basis[...])
+    a1[r] = jnp.zeros((2, 128), F32)
+    a1[r, :, 0:n_all] = fresh[4:6, :]
+    a1[r, :, 64 : 64 + n_all] = fresh[6:8, :]
 
     @pl.loop(0, n_row - 1)
     def _(i):
@@ -313,7 +332,7 @@
     part = a2[0]
     for i in range(1, n_col):
         part = part + a2[i]
-    fresh = part[:, 0:n_all] * scale
+    fresh = jnp.concatenate([jnp.zeros((4, n_all), F32), part[:, 0:n_all], part[:, 64 : 64 + n_all]], axis=0) * scale
     proj[...] = base + dot_nn(dot_nt(inverse, fresh), last)
     out_proj = pltpu.make_async_copy(proj, proj_o, loc.at[2])
     out_proj.start()
@@ -322,15 +341,15 @@
     out_image.wait()
 
 
-def hand_out(a_in, b_in, c_in, a_out, b_out, c_out, a, b, c, sem):
-    loads = [pltpu.make_async_copy(x, y, sem.at[i]) for i, (x, y) in enumerate(((a_in, a), (b_in, b), (c_in, c)))]
-    stores = [pltpu.make_async_copy(x, y, sem.at[3 + i]) for i, (x, y) in enumerate(((a, a_out), (b, b_out), (c, c_out)))]
-    for copy in loads:
+def hand_out(a_in, b_in, c_in, a_out, b_out, c_out, sem):
+    copies = [
+        pltpu.make_async_copy(b_in, b_out, sem.at[0]),
+        pltpu.make_async_copy(c_in, c_out, sem.at[1]),
+        pltpu.make_async_copy(a_in, a_out, sem.at[2]),
+    ]
+    for copy in copies:
         copy.start()
-    for load, store in zip(loads, stores):
-        load.wait()
-        store.start()
-    for copy in stores:
+    for copy in copies:
         copy.wait()
 
 
@@ -343,6 +362,10 @@
     n_all = n_old + n_vec
     hbm = pl.BlockSpec(memory_space=pltpu.HBM)
     v = pltpu.VMEM
+    operands = [
+        pltpu.with_memory_space_constraint(x, pltpu.HBM)
+        for x in (tile_rows, tile_cols, tile_blocks, trial_vectors, basis_old, image_old)
+    ]
     outs = pl.pallas_call(
         functools.partial(kernel, n_row, n_col, float(width * n_row * n_col)),
         out_shape=(
@@ -351,7 +374,7 @@
             jax.ShapeDtypeStruct((n_all, width), F32),
         ),
         in_specs=[hbm] * 6,
-        out_specs=(hbm, hbm, hbm),
+        out_specs=(pl.BlockSpec(memory_space=pl.ANY),) * 3,
         scratch_shapes=[
             pltpu.SMEM((kt,), jnp.int32),
             pltpu.SMEM((kt,), jnp.int32),
@@ -375,25 +398,26 @@
             v((n_row, 8, 128), F32),
             v((n_col, 8, 128), F32),
             v((n_all // 8, 8, 128), F32),
-            v((n_row, 8, 128), F32),
-            v((n_col, 8, 128), F32),
+            v((n_row, 2, 128), F32),
+            v((n_col, 2, 128), F32),
             v((n_all, width), F32),
             v((n_all, width), F32),
             v((n_all, n_all), F32),
             pltpu.SemaphoreType.DMA((6,)),
             pltpu.SemaphoreType.DMA((12, 2)),
+            pltpu.SemaphoreType.DMA((n_row // 2,)),
         ],
         compiler_params=pltpu.CompilerParams(
-            collective_id=0, has_side_effects=True, vmem_limit_bytes=60 << 20
+            collective_id=0, has_side_effects=True, vmem_limit_bytes=32 << 20
         ),
-    )(tile_rows, tile_cols, tile_blocks, trial_vectors, basis_old, image_old)
+    )(*operands)
     return pl.pallas_call(
         hand_out,
         out_shape=tuple(jax.ShapeDtypeStruct(o.shape, o.dtype) for o in outs),
-        in_specs=[hbm] * 3,
+        in_specs=[pl.BlockSpec(memory_space=pl.ANY)] * 3,
         out_specs=(hbm,) * 3,
-        scratch_shapes=[v(o.shape, o.dtype) for o in outs] + [pltpu.SemaphoreType.DMA((6,))],
-        compiler_params=pltpu.CompilerParams(vmem_limit_bytes=60 << 20),
+        scratch_shapes=[pltpu.SemaphoreType.DMA((3,))],
+        compiler_params=pltpu.CompilerParams(vmem_limit_bytes=32 << 20),
     )(*outs)
 
 

time: 52 us -> 48.5 us (0.933)
  Pallas kernels: 51.2 us -> 47.7 us
    pallas_call x1, Pallas kernels: 49.4 us -> 47 us  [local(): pl.pallas_call(functools.partial(kernel, n_row, n_col, float(width * n_ro...]
    pallas_call x1, Pallas kernels: 1.77 us -> 0.77 us  [local(): pl.pallas_call(hand_out, out_shape=tuple((jax.ShapeDtypeStruct(o.shape, o...]
where the time goes in v4:
time: 48.5 us; the launch traced here: 48.4 us
  Pallas kernels  47.7 us (98%)
  between operations  0.64 us (1%)
    pallas_call x1, Pallas kernels, local(): pl.pallas_call(functools.partial(kernel, n_row, n_col, float(width * n_ro...  47 us

profile of v4, /device:TPU:1, one launch (start us, length us, event | category | flops | bytes accessed | tf_op | source)
XLA Modules:
  0.0 48.4 jit_solution(7748731970513934125)
XLA Ops:
  0.6 47.0 %shard_map.85 = (f32[48,48]{1,0:T(8,128)S(1)}, f32[48,1024]{1,0:T(8,128)S(1)}, f32[48,1024]{1,0:T(8,128)S(1)}) custom-call(s32[24]{0:T(128)} %rows_h.1, s32[24]{0:T(128)} %cols_h.1, bf16[24,128,128]{2,1,0:T(8,128)(2,1)} %tiles_h.1, bf16[4,1024]{1,0:T(4,128)(2,1)} %trial_h.1, f32[44,1024]{1,0:T(8,128)} %basis_h.1, f32[44,1024]{1,0:T(8,128)} %image_h.1), custom_call_target="tpu_custom_call" | custom-call | tf_op jit(solution)/shard_map/pallas_call | solution.py:369
  47.6 0.8 %shard_map.86 = (f32[48,48]{1,0:T(8,128)}, f32[48,1024]{1,0:T(8,128)}, f32[48,1024]{1,0:T(8,128)}) custom-call(f32[48,48]{1,0:T(8,128)S(1)} %get-tuple-element.6.a_in, f32[48,1024]{1,0:T(8,128)S(1)} %get-tuple-element.7.b_in, f32[48,1024]{1,0:T(8,128)S(1)} %get-tuple-element.8.c_in), custom_call_target="tpu_custom_call" | custom-call | tf_op jit(solution)/shard_map/pallas_call | solution.py:414

commit v5 on v4

--- a/solution.py
+++ b/solution.py
@@ -53,7 +53,7 @@
     rows_h, cols_h, tiles_h, trial_h, basis_h, image_h,
     proj_o, basis_o, image_o,
     rows_s, cols_s, tiles, trial, old_basis, old_image, basis, image, mix,
-    x_row, x_col, prod, prod2, keys, row_send, col_send, row_recv, col_recv,
+    x_row, x_col, prod, prod2, keys, pick_row, pick_col, row_send, col_send, row_recv, col_recv,
     gram, e1, e2, sums, a1, a2, new_basis, new_image, proj,
     loc, sem, relay,
 ):
@@ -169,20 +169,34 @@
         def _():
             rcopy(gram.at[p], e1.at[r], 2, (p * step, c)).start()
 
+    drain(keys.at[1], 10)
+    key = jnp.concatenate([jnp.concatenate([keys[0]] * 2 + [keys[1]] * 2, axis=1)] * 16, axis=0)
+    at = lax.broadcasted_iota(jnp.int32, (128, 512), 0)
+    at = (at // 32 * 2 + core) * 32 + at % 32
+
+    @pl.loop(0, half // 4)
+    def _(s):
+        pick_row[s] = jnp.where(at + s * 256 == key, 1.0, 0.0).astype(BF16)
+
+    key2 = jnp.concatenate([jnp.concatenate([row_key] * 2, axis=1)] * 16, axis=0)
+    at2 = lax.broadcasted_iota(jnp.int32, (128, 256), 0)
+
+    @pl.loop(0, n_col // 4)
+    def _(s):
+        pick_col[s] = jnp.where(at2 + s * 128 == key2, 1.0, 0.0).astype(BF16)
+
     local[3].wait()
     prod[...] = jnp.zeros(prod.shape, F32)
 
     def products(which, x, index, along):
-        @pl.loop(0, kt // 4)
-        def _(s):
+        if True:
             out = []
-            for u in range(4):
-                t = s * 4 + u
+            for t in range(kt):
                 out.append(
                     lax.dot_general(
                         x[index(t)], tiles[t], (((1,), (along,)), ((), ())), preferred_element_type=F32)
                 )
-            prod[which, pl.ds(pl.multiple_of(s * 16, 16), 16), :] = jnp.concatenate(out, axis=0)
+            prod[which, 0 : 4 * kt, :] = jnp.concatenate(out, axis=0)
 
     def split(p):
         high = p.astype(BF16)
@@ -221,18 +235,12 @@
         ).wait_recv()
         rcopy(piece_in, piece_in, 7, twin).start()
 
-    drain(keys.at[1], 10)
     drain(prod2, 11)
     both = jnp.concatenate([*split(prod[1]), *split(prod2[...])], axis=0)
-    key = jnp.concatenate([jnp.concatenate([keys[0]] * 2 + [keys[1]] * 2, axis=1)] * 16, axis=0)
-    at = lax.broadcasted_iota(jnp.int32, (128, 512), 0)
-    at = (at // 32 * 2 + core) * 32 + at % 32
-
-    @pl.loop(0, n_row // 8)
-    def _(s):
-        pick = jnp.where(at + s * 256 == key, 1.0, 0.0).astype(BF16)
-        placed = lax.dot_general(pick, both, (((1,), (0,)), ((), ())), preferred_element_type=F32)
-        row_send[pl.ds(s * 4, 4)] = placed.reshape(4, 32, 128)
+
+    for s in range(half // 4):
+        placed = lax.dot_general(pick_row[s], both, (((1,), (0,)), ((), ())), preferred_element_type=F32)
+        row_send[4 * s : 4 * s + 4] = placed.reshape(4, 32, 128)
 
     @pl.loop(0, half - 1)
     def _(i):
@@ -245,14 +253,10 @@
     rcopy(sent, sent, 0, (r, c)).wait_send()
     products(0, x_row, col_of, 1)
     both = jnp.concatenate(split(prod[0]), axis=0)
-    key = jnp.concatenate([jnp.concatenate([row_key] * 2, axis=1)] * 16, axis=0)
-    at = lax.broadcasted_iota(jnp.int32, (128, 256), 0)
-
-    @pl.loop(0, n_col // 4)
-    def _(s):
-        pick = jnp.where(at + s * 128 == key, 1.0, 0.0).astype(BF16)
-        placed = lax.dot_general(pick, both, (((1,), (0,)), ((), ())), preferred_element_type=F32)
-        col_send[pl.ds(s * 4, 4)] = placed.reshape(4, 32, 128)
+
+    for s in range(n_col // 4):
+        placed = lax.dot_general(pick_col[s], both, (((1,), (0,)), ((), ())), preferred_element_type=F32)
+        col_send[4 * s : 4 * s + 4] = placed.reshape(4, 32, 128)
 
     @pl.loop(0, n_col - 1)
     def _(i):
@@ -390,6 +394,8 @@
             v((2, 128, ts), F32),
             v((128, ts), F32),
             v((2, 8, 128), jnp.int32),
+            v((n_row // 8, 128, 512), BF16),
+            v((n_col // 4, 128, 256), BF16),
             v((n_row // 2, 32, ts), F32),
             v((n_col, 32, ts), F32),
             v((n_row // 2 - 1, 32, ts), F32),

time: 48.5 us -> 47.5 us (0.979)
  Pallas kernels: 47.7 us -> 46.6 us
    pallas_call x1, Pallas kernels: 47 us -> 45.9 us  [local(): pl.pallas_call(functools.partial(kernel, n_row, n_col, float(width * n_ro...]
where the time goes in v5:
time: 47.5 us; the launch traced here: 47.3 us
  Pallas kernels  46.6 us (98%)
  between operations  0.64 us (1%)
    pallas_call x1, Pallas kernels, local(): pl.pallas_call(functools.partial(kernel, n_row, n_col, float(width * n_ro...  45.9 us

profile of v5, /device:TPU:1, one launch (start us, length us, event | category | flops | bytes accessed | tf_op | source)
XLA Modules:
  0.0 47.3 jit_solution(9414585701719339985)
XLA Ops:
  0.6 45.9 %shard_map.85 = (f32[48,48]{1,0:T(8,128)S(1)}, f32[48,1024]{1,0:T(8,128)S(1)}, f32[48,1024]{1,0:T(8,128)S(1)}) custom-call(s32[24]{0:T(128)} %rows_h.1, s32[24]{0:T(128)} %cols_h.1, bf16[24,128,128]{2,1,0:T(8,128)(2,1)} %tiles_h.1, bf16[4,1024]{1,0:T(4,128)(2,1)} %trial_h.1, f32[44,1024]{1,0:T(8,128)} %basis_h.1, f32[44,1024]{1,0:T(8,128)} %image_h.1), custom_call_target="tpu_custom_call" | custom-call | tf_op jit(solution)/shard_map/pallas_call | solution.py:373
  46.5 0.8 %shard_map.86 = (f32[48,48]{1,0:T(8,128)}, f32[48,1024]{1,0:T(8,128)}, f32[48,1024]{1,0:T(8,128)}) custom-call(f32[48,48]{1,0:T(8,128)S(1)} %get-tuple-element.6.a_in, f32[48,1024]{1,0:T(8,128)S(1)} %get-tuple-element.7.b_in, f32[48,1024]{1,0:T(8,128)S(1)} %get-tuple-element.8.c_in), custom_call_target="tpu_custom_call" | custom-call | tf_op jit(solution)/shard_map/pallas_call | solution.py:420

commit v6 on v5

--- a/solution.py
+++ b/solution.py
@@ -21,7 +21,7 @@
     return lax.dot_general(a, b, (((1,), (0,)), ((), ())), precision=HIGHEST, preferred_element_type=F32)
 
 
-def lower_inverse(a):
+def lower_inverse(a, pause):
     n = a.shape[0]
     tiles = n // 8
     sub = lax.broadcasted_iota(jnp.int32, (8, n), 0)
@@ -29,6 +29,8 @@
     left = [a[8 * i : 8 * i + 8, :] for i in range(tiles)]
     right = [jnp.where(sub + 8 * i == lane, 1.0, 0.0).astype(F32) for i in range(tiles)]
     for j in range(n):
+        if j == n * 3 // 4:
+            pause()
         at, row = j // 8, j % 8
         pivot_left = left[at][row : row + 1, :]
         pivot_right = right[at][row : row + 1, :]
@@ -112,7 +114,7 @@
     @pl.loop(0, n_col - 1)
     def _(i):
         own = pl.ds(c * 8, 8)
-        rcopy(x_col.at[own], x_col.at[own], 1, (r, lax.rem(c + far_first(i, n_col), n_col))).start()
+        rcopy(x_col.at[own], x_col.at[own], 1, (r, lax.rem(c // 8 + 1 - i % 2, 2) * 8 + lax.rem(c % 8 + far_first(i // 2, 8), 8))).start()
 
     half = n_row // 2
     pair = r // 2
@@ -309,19 +311,20 @@
 
     scale = 1.0 / total_cols
     g = jnp.concatenate([sums[i] for i in range(pieces)], axis=0) * scale
-    inverse = lower_inverse(g[:, 0:n_all])
+    def pass_on():
+
+        drain(a1.at[pl.ds(0, n_row - 1)], 8)
+        part = a1[0]
+        for i in range(1, n_row):
+            part = part + a1[i]
+        a2[c] = part
+
+        @pl.loop(0, n_col - 1)
+        def _(i):
+            rcopy(a2.at[c], a2.at[c], 9, (r, lax.rem(c // 8 + 1 - i % 2, 2) * 8 + lax.rem(c % 8 + far_first(i // 2, 8), 8))).start()
+
+    inverse = lower_inverse(g[:, 0:n_all], pass_on)
     old_coupling = g[:, n_all : 2 * n_all]
-
-    drain(a1.at[pl.ds(0, n_row - 1)], 8)
-    part = a1[0]
-    for i in range(1, n_row):
-        part = part + a1[i]
-    a2[c] = part
-
-    @pl.loop(0, n_col - 1)
-    def _(i):
-        rcopy(a2.at[c], a2.at[c], 9, (r, lax.rem(c + far_first(i, n_col), n_col))).start()
-
     new_basis[...] = dot_nn(inverse, basis[...])
     out_basis = pltpu.make_async_copy(new_basis, basis_o, loc.at[0])
     out_basis.start()

time: 47.5 us -> 47.2 us (level)
  no operation moved by 1% of the time
where the time goes in v6:
time: 47.2 us; the launch traced here: 47 us
  Pallas kernels  46.4 us (98%)
  between operations  0.64 us (1%)
    pallas_call x1, Pallas kernels, local(): pl.pallas_call(functools.partial(kernel, n_row, n_col, float(width * n_ro...  45.6 us

profile of v6, /device:TPU:1, one launch (start us, length us, event | category | flops | bytes accessed | tf_op | source)
XLA Modules:
  0.0 47.0 jit_solution(15671251970901955399)
XLA Ops:
  0.6 45.6 %shard_map.85 = (f32[48,48]{1,0:T(8,128)S(1)}, f32[48,1024]{1,0:T(8,128)S(1)}, f32[48,1024]{1,0:T(8,128)S(1)}) custom-call(s32[24]{0:T(128)} %rows_h.1, s32[24]{0:T(128)} %cols_h.1, bf16[24,128,128]{2,1,0:T(8,128)(2,1)} %tiles_h.1, bf16[4,1024]{1,0:T(4,128)(2,1)} %trial_h.1, f32[44,1024]{1,0:T(8,128)} %basis_h.1, f32[44,1024]{1,0:T(8,128)} %image_h.1), custom_call_target="tpu_custom_call" | custom-call | tf_op jit(solution)/shard_map/pallas_call | solution.py:376
  46.3 0.8 %shard_map.86 = (f32[48,48]{1,0:T(8,128)}, f32[48,1024]{1,0:T(8,128)}, f32[48,1024]{1,0:T(8,128)}) custom-call(f32[48,48]{1,0:T(8,128)S(1)} %get-tuple-element.6.a_in, f32[48,1024]{1,0:T(8,128)S(1)} %get-tuple-element.7.b_in, f32[48,1024]{1,0:T(8,128)S(1)} %get-tuple-element.8.c_in), custom_call_target="tpu_custom_call" | custom-call | tf_op jit(solution)/shard_map/pallas_call | solution.py:423

commit v7 on v6

--- a/solution.py
+++ b/solution.py
@@ -29,7 +29,7 @@
     left = [a[8 * i : 8 * i + 8, :] for i in range(tiles)]
     right = [jnp.where(sub + 8 * i == lane, 1.0, 0.0).astype(F32) for i in range(tiles)]
     for j in range(n):
-        if j == n * 3 // 4:
+        if j == n * 7 // 8:
             pause()
         at, row = j // 8, j % 8
         pivot_left = left[at][row : row + 1, :]

time: 47.2 us -> 47.2 us (level)
  no operation moved by 1% of the time
where the time goes in v7:
time: 47.2 us; the launch traced here: 47 us
  Pallas kernels  46.4 us (98%)
  between operations  0.64 us (1%)
    pallas_call x1, Pallas kernels, local(): pl.pallas_call(functools.partial(kernel, n_row, n_col, float(width * n_ro...  45.6 us

profile of v7, /device:TPU:1, one launch (start us, length us, event | category | flops | bytes accessed | tf_op | source)
XLA Modules:
  0.0 47.0 jit_solution(14152070998414448706)
XLA Ops:
  0.6 45.6 %shard_map.85 = (f32[48,48]{1,0:T(8,128)S(1)}, f32[48,1024]{1,0:T(8,128)S(1)}, f32[48,1024]{1,0:T(8,128)S(1)}) custom-call(s32[24]{0:T(128)} %rows_h.1, s32[24]{0:T(128)} %cols_h.1, bf16[24,128,128]{2,1,0:T(8,128)(2,1)} %tiles_h.1, bf16[4,1024]{1,0:T(4,128)(2,1)} %trial_h.1, f32[44,1024]{1,0:T(8,128)} %basis_h.1, f32[44,1024]{1,0:T(8,128)} %image_h.1), custom_call_target="tpu_custom_call" | custom-call | tf_op jit(solution)/shard_map/pallas_call | solution.py:376
  46.3 0.8 %shard_map.86 = (f32[48,48]{1,0:T(8,128)}, f32[48,1024]{1,0:T(8,128)}, f32[48,1024]{1,0:T(8,128)}) custom-call(f32[48,48]{1,0:T(8,128)S(1)} %get-tuple-element.6.a_in, f32[48,1024]{1,0:T(8,128)S(1)} %get-tuple-element.7.b_in, f32[48,1024]{1,0:T(8,128)S(1)} %get-tuple-element.8.c_in), custom_call_target="tpu_custom_call" | custom-call | tf_op jit(solution)/shard_map/pallas_call | solution.py:423
